TPU v7x, 32 devices: a whole 2x2x4 slice. The times are simulated.
32 devices in a mesh: rep: 4 (over y, core), seq: 2 (over x), ctx: 4 (over z).
Axes of the slice: x: 2, y: 2, z: 4, core: 2. Of those that a mesh axis runs over, the one named last changes fastest.
Arguments:
- tokens: bfloat16 [8192, 2048], P(('rep', 'seq', 'ctx')), may hold values from -6 to 6
- cotangent: bfloat16 [8192, 2048], P(('rep', 'seq', 'ctx')), may hold values from -6 to 6
- document_index: int32 [8192], P(('rep', 'seq')), may hold values from 0 to 10, as said below
- padding_token_mask: int32 [8192], P(('rep', 'seq')), may hold values from 0 to 1, as said below
- attention_gain: bfloat16 [2048], P(('seq', 'ctx')), may hold values from 0.099609375 to 1.8984375
- projection_weight: bfloat16 [2048, 6144], P(('seq', 'ctx')), may hold values from -0.125 to 0.125
- head_gain: bfloat16 [2, 128], replicated, may hold values from 0.099609375 to 1.8984375
- out_weight: bfloat16 [2048, 2048], P(('seq', 'ctx')), may hold values from -2 to 2
- feedforward_gain: bfloat16 [2048], P(('seq', 'ctx')), may hold values from 0.099609375 to 1.8984375
- gate_weight: bfloat16 [2048, 6144], P(('seq', 'ctx')), may hold values from -0.125 to 0.125
- up_weight: bfloat16 [2048, 6144], P(('seq', 'ctx')), may hold values from -0.125 to 0.125
- down_weight: bfloat16 [2048, 6144], P(('seq', 'ctx')), may hold values from -0.078125 to 0.078125
Outputs:
- layer_out: bfloat16 [8192, 2048], P(('rep', 'seq', 'ctx'))
- tokens_grad: bfloat16 [8192, 2048], P(('rep', 'seq', 'ctx'))
- attention_gain_grad: float32 [2048], P(('seq', 'ctx'))
- proj_weight_grad: float32 [2048, 6144], P(('seq', 'ctx'))
- head_gain_grad: float32 [2, 128], replicated
- out_weight_grad: float32 [2048, 2048], P(('seq', 'ctx'))
- feedforward_gain_grad: float32 [2048], P(('seq', 'ctx'))
- gate_weight_grad: float32 [2048, 6144], P(('seq', 'ctx'))
- up_weight_grad: float32 [2048, 6144], P(('seq', 'ctx'))
- down_weight_grad: float32 [2048, 6144], P(('seq', 'ctx'))
Inputs may be any that keep to these rules, and one draw needn't show every extreme that they name: `document_index`: along each sequence of 1024 tokens the ids never fall. `padding_token_mask`: the zeros of a sequence form one run at its end.
All inputs are finite; a program needn't handle non-finite values.
Results may differ from a plain program's by a relative error of at most 0.02.
Values may be sent and summed in bfloat16 or wider, within the bound.
A program may use at most 640 MiB of HBM per device.

v0:
```python
import jax
import jax.numpy as jnp
from jax import lax
from jax.sharding import PartitionSpec as P

QUERY_HEADS = 16
KEY_VALUE_HEADS = 8
HEAD_SIZE = 128
norm_epsilon = 1e-06
rope_base = 1000000.0
masked_value = -1e30
contract_rows = (((0,), (0,)), ((), ()))
contract_cols = (((1,), (1,)), ((), ()))


def rope_tables(positions):
    half_size = HEAD_SIZE // 2
    frequency = rope_base ** (-2.0 * jnp.arange(half_size, dtype=jnp.float32) / HEAD_SIZE)
    angles = positions.astype(jnp.float32)[:, None, None] * frequency[None, None, :]
    return (jnp.cos(angles), jnp.sin(angles))


def rotate(value_rows, cosine_table, sine_table):
    half_size = value_rows.shape[-1] // 2
    first_half = value_rows[..., :half_size]
    second_half = value_rows[..., half_size:]
    return jnp.concatenate(
        [
            first_half * cosine_table - second_half * sine_table,
            second_half * cosine_table + first_half * sine_table,
        ],
        axis=-1,
    )


def inverse_rotation(grads, cosine_table, sine_table):
    half_size = grads.shape[-1] // 2
    first_half = grads[..., :half_size]
    second_half = grads[..., half_size:]
    return jnp.concatenate(
        [
            first_half * cosine_table + second_half * sine_table,
            second_half * cosine_table - first_half * sine_table,
        ],
        axis=-1,
    )


def head_norm(value_rows, gain):
    root_factor = lax.rsqrt(
        jnp.mean(value_rows * value_rows, axis=-1, keepdims=True) + norm_epsilon
    )
    unit_values = value_rows * root_factor
    return (unit_values * gain, unit_values, root_factor)


def norm_back(grad_out, unit_values, root_factor, gain):
    scaled = grad_out * gain
    return root_factor * (
        scaled - unit_values * jnp.mean(scaled * unit_values, axis=-1, keepdims=True)
    )


def over_replicas(grad_parts):
    return (
        lax.psum(grad_parts[0].astype(jnp.bfloat16), "rep").astype(jnp.float32),
        lax.psum(grad_parts[1].astype(jnp.bfloat16), "rep").astype(jnp.float32),
    )


def per_device(
    tokens,
    cotangent,
    document_index,
    padding_token_mask,
    attention_gain,
    projection_weight,
    head_gain,
    out_weight,
    feedforward_gain,
    gate_weight,
    up_weight,
    down_weight,
):
    token_rows = tokens.shape[0]
    sequence_length = document_index.shape[0]
    shard_rows = projection_weight.shape[0]
    proj_width = projection_weight.shape[1]
    ff_width = gate_weight.shape[1]
    query_total_width = QUERY_HEADS * HEAD_SIZE
    key_total_width = KEY_VALUE_HEADS * HEAD_SIZE
    query_group_width = QUERY_HEADS // KEY_VALUE_HEADS
    score_scale = HEAD_SIZE ** (-0.5)
    tokens_wide = tokens.astype(jnp.float32)
    root_attn = lax.rsqrt(jnp.mean(tokens_wide * tokens_wide, axis=1, keepdims=True) + norm_epsilon)
    unit_attn = tokens_wide * root_attn
    gain_piece = lax.all_gather(attention_gain, ("seq", "ctx"), axis=0, tiled=True)
    weight_piece = lax.all_gather(projection_weight, ("seq", "ctx"), axis=0, tiled=True)
    columns = unit_attn
    normed = (columns * gain_piece.astype(jnp.float32)).astype(jnp.bfloat16)
    result = (
        jnp.dot(normed, weight_piece, preferred_element_type=jnp.float32),
        gain_piece.astype(jnp.float32),
        normed,
    )
    folded_proj = result
    projected_rows = folded_proj[0]
    gain_attn_full = folded_proj[1]
    normed_attn = folded_proj[2]
    queries_raw = projected_rows[:, :query_total_width].reshape(token_rows, QUERY_HEADS, HEAD_SIZE)
    gate_logits = projected_rows[:, query_total_width : 2 * query_total_width]
    keys_raw = projected_rows[
        :, 2 * query_total_width : 2 * query_total_width + key_total_width
    ].reshape(token_rows, KEY_VALUE_HEADS, HEAD_SIZE)
    values_raw = projected_rows[:, 2 * query_total_width + key_total_width :]
    first_row = lax.axis_index("ctx") * token_rows
    positions = first_row + jnp.arange(token_rows, dtype=jnp.int32)
    cosine_table, sine_table = rope_tables(positions)
    head_gain_wide = head_gain.astype(jnp.float32)
    query_normed, query_unit, query_root = head_norm(queries_raw, head_gain_wide[0])
    key_normed, key_unit, key_root = head_norm(keys_raw, head_gain_wide[1])
    query_low = (
        rotate(query_normed, cosine_table, sine_table)
        .astype(jnp.bfloat16)
        .reshape(token_rows, KEY_VALUE_HEADS, query_group_width, HEAD_SIZE)
    )
    key_low = (
        rotate(key_normed, cosine_table, sine_table)
        .astype(jnp.bfloat16)
        .reshape(token_rows, key_total_width)
    )
    value_low = values_raw.astype(jnp.bfloat16)
    every_key, every_value = (
        lax.all_gather(key_low, "ctx", axis=0, tiled=True),
        lax.all_gather(value_low, "ctx", axis=0, tiled=True),
    )
    every_key = every_key.reshape(sequence_length, KEY_VALUE_HEADS, HEAD_SIZE)
    every_value = every_value.reshape(sequence_length, KEY_VALUE_HEADS, HEAD_SIZE)
    seg_here = lax.dynamic_slice_in_dim(document_index, first_row, token_rows, 0)
    pad_here = lax.dynamic_slice_in_dim(padding_token_mask, first_row, token_rows, 0)
    key_places = jnp.arange(sequence_length, dtype=jnp.int32)
    allowed = (seg_here[:, None] == document_index[None, :]) & (
        key_places[None, :] <= positions[:, None]
    ) & (padding_token_mask[None, :] == 1) | (key_places[None, :] == positions[:, None])

    def masked_scores():
        raw_scores = (
            jnp.einsum("qhgd,khd->hgqk", query_low, every_key, preferred_element_type=jnp.float32)
            * score_scale
        )
        return jnp.where(allowed[None, None], raw_scores, masked_value)

    scores = masked_scores()
    peak = jnp.max(scores, axis=3, keepdims=True)
    exp_scores = jnp.exp(scores - peak)
    denominator = jnp.sum(exp_scores, axis=3, keepdims=True)
    log_total = peak + jnp.log(denominator)
    probs_low = (exp_scores / denominator).astype(jnp.bfloat16)
    attended_rows = jnp.einsum(
        "hgqk,khd->qhgd", probs_low, every_value, preferred_element_type=jnp.float32
    ).reshape(token_rows, query_total_width)
    gate_activations = jax.nn.sigmoid(gate_logits)
    mixed_heads = (attended_rows * gate_activations).astype(jnp.bfloat16)
    columns = lax.dot_general(
        mixed_heads,
        lax.all_gather(out_weight, ("seq", "ctx"), axis=0, tiled=True),
        contract_cols,
        preferred_element_type=jnp.float32,
    )
    result = (columns,)
    folded_out = result
    resid_mid = tokens_wide + folded_out[0]
    root_mlp = lax.rsqrt(jnp.mean(resid_mid * resid_mid, axis=1, keepdims=True) + norm_epsilon)
    unit_mlp = resid_mid * root_mlp
    gain_piece = lax.all_gather(feedforward_gain, ("seq", "ctx"), axis=0, tiled=True)
    gate_piece = lax.all_gather(gate_weight, ("seq", "ctx"), axis=0, tiled=True)
    up_piece = lax.all_gather(up_weight, ("seq", "ctx"), axis=0, tiled=True)
    columns = unit_mlp
    normed = (columns * gain_piece.astype(jnp.float32)).astype(jnp.bfloat16)
    result = (
        jnp.dot(normed, gate_piece, preferred_element_type=jnp.float32),
        jnp.dot(normed, up_piece, preferred_element_type=jnp.float32),
        gain_piece.astype(jnp.float32),
        normed,
    )
    folded_mlp = result
    gate_lin = folded_mlp[0]
    up_lin = folded_mlp[1]
    gain_mlp_full = folded_mlp[2]
    normed_mlp = folded_mlp[3]
    gate_sig = jax.nn.sigmoid(gate_lin)
    silu_gate = gate_lin * gate_sig
    hidden_low = (silu_gate * up_lin).astype(jnp.bfloat16)
    columns = lax.dot_general(
        hidden_low,
        lax.all_gather(down_weight, ("seq", "ctx"), axis=0, tiled=True),
        contract_cols,
        preferred_element_type=jnp.float32,
    )
    result = (columns,)
    layer_out = (resid_mid + result[0]).astype(jnp.bfloat16)
    masked_grad = cotangent.astype(jnp.float32) * pad_here.astype(jnp.float32)[:, None]
    d_out_low = masked_grad.astype(jnp.bfloat16)
    columns = d_out_low
    d_hidden = jnp.dot(
        columns,
        lax.all_gather(down_weight, ("seq", "ctx"), axis=0, tiled=True),
        preferred_element_type=jnp.float32,
    )
    d_gate_low = (d_hidden * up_lin * gate_sig * (1.0 + gate_lin * (1.0 - gate_sig))).astype(
        jnp.bfloat16
    )
    d_up_low = (d_hidden * silu_gate).astype(jnp.bfloat16)
    gate_piece = lax.all_gather(gate_weight, ("seq", "ctx"), axis=0, tiled=True)
    up_piece = lax.all_gather(up_weight, ("seq", "ctx"), axis=0, tiled=True)
    columns = lax.dot_general(
        d_gate_low, gate_piece, contract_cols, preferred_element_type=jnp.float32
    ) + lax.dot_general(d_up_low, up_piece, contract_cols, preferred_element_type=jnp.float32)
    d_normed_mlp = columns
    normed_rows = normed_mlp
    grad_rows = d_out_low
    mlp_grads = lax.psum_scatter(
        jnp.concatenate(
            [
                lax.dot_general(
                    normed_rows, d_gate_low, contract_rows, preferred_element_type=jnp.float32
                ),
                lax.dot_general(
                    normed_rows, d_up_low, contract_rows, preferred_element_type=jnp.float32
                ),
                lax.dot_general(
                    grad_rows, hidden_low, contract_rows, preferred_element_type=jnp.float32
                ),
            ],
            axis=1,
        ).astype(jnp.bfloat16),
        ("seq", "ctx"),
        scatter_dimension=0,
        tiled=True,
    ).astype(jnp.float32)
    gain_mlp_term = jnp.sum(d_normed_mlp * unit_mlp, axis=0)
    d_resid_mid = masked_grad + norm_back(d_normed_mlp, unit_mlp, root_mlp, gain_mlp_full)
    d_attn_low = d_resid_mid.astype(jnp.bfloat16)
    columns = d_attn_low
    mixed_gradient = jnp.dot(
        columns,
        lax.all_gather(out_weight, ("seq", "ctx"), axis=0, tiled=True),
        preferred_element_type=jnp.float32,
    )
    d_gate_logits = mixed_gradient * attended_rows * gate_activations * (1.0 - gate_activations)
    d_attended_low = (
        (mixed_gradient * gate_activations)
        .astype(jnp.bfloat16)
        .reshape(token_rows, KEY_VALUE_HEADS, query_group_width, HEAD_SIZE)
    )
    probs = jnp.exp(masked_scores() - log_total)
    d_probs = jnp.einsum(
        "qhgd,khd->hgqk", d_attended_low, every_value, preferred_element_type=jnp.float32
    )
    value_term = jnp.einsum(
        "hgqk,qhgd->khd", probs_low, d_attended_low, preferred_element_type=jnp.float32
    )
    delta = jnp.sum(probs * d_probs, axis=3, keepdims=True)
    d_scores_low = (probs * (d_probs - delta)).astype(jnp.bfloat16)
    d_queries = (
        jnp.einsum("hgqk,khd->qhgd", d_scores_low, every_key, preferred_element_type=jnp.float32)
        * score_scale
    )
    key_term = (
        jnp.einsum("hgqk,qhgd->khd", d_scores_low, query_low, preferred_element_type=jnp.float32)
        * score_scale
    )
    key_gradient, d_values = (
        lax.psum_scatter(
            key_term.reshape(sequence_length, key_total_width).astype(jnp.bfloat16),
            "ctx",
            scatter_dimension=0,
            tiled=True,
        ).astype(jnp.float32),
        lax.psum_scatter(
            value_term.reshape(sequence_length, key_total_width).astype(jnp.bfloat16),
            "ctx",
            scatter_dimension=0,
            tiled=True,
        ).astype(jnp.float32),
    )
    d_query_normed = inverse_rotation(
        d_queries.reshape(token_rows, QUERY_HEADS, HEAD_SIZE), cosine_table, sine_table
    )
    normed_key_gradient = inverse_rotation(
        key_gradient.reshape(token_rows, KEY_VALUE_HEADS, HEAD_SIZE), cosine_table, sine_table
    )
    head_term = jnp.stack(
        [
            jnp.sum(d_query_normed * query_unit, axis=(0, 1)),
            jnp.sum(normed_key_gradient * key_unit, axis=(0, 1)),
        ]
    )
    d_query_raw = norm_back(d_query_normed, query_unit, query_root, head_gain_wide[0])
    d_key_raw = norm_back(normed_key_gradient, key_unit, key_root, head_gain_wide[1])
    d_proj_low = jnp.concatenate(
        [
            d_query_raw.reshape(token_rows, query_total_width),
            d_gate_logits,
            d_key_raw.reshape(token_rows, key_total_width),
            d_values,
        ],
        axis=1,
    ).astype(jnp.bfloat16)
    columns = lax.dot_general(
        d_proj_low,
        lax.all_gather(projection_weight, ("seq", "ctx"), axis=0, tiled=True),
        contract_cols,
        preferred_element_type=jnp.float32,
    )
    normed_rows = normed_attn
    grad_rows = d_attn_low
    attn_grads = lax.psum_scatter(
        jnp.concatenate(
            [
                lax.dot_general(
                    normed_rows, d_proj_low, contract_rows, preferred_element_type=jnp.float32
                ),
                lax.dot_general(
                    grad_rows, mixed_heads, contract_rows, preferred_element_type=jnp.float32
                ),
            ],
            axis=1,
        ).astype(jnp.bfloat16),
        ("seq", "ctx"),
        scatter_dimension=0,
        tiled=True,
    ).astype(jnp.float32)
    gain_attn_term = jnp.sum(columns * unit_attn, axis=0)
    tokens_grad = (d_resid_mid + norm_back(columns, unit_attn, root_attn, gain_attn_full)).astype(
        jnp.bfloat16
    )
    sum_attn_gain, sum_mlp_gain, sum_head_gain = lax.psum(
        (gain_attn_term, gain_mlp_term, head_term), ("rep", "seq", "ctx")
    )
    mlp_grads, attn_grads = over_replicas((mlp_grads, attn_grads))
    group_rank = lax.axis_index(("seq", "ctx"))
    attention_gain_grad = lax.dynamic_slice_in_dim(
        sum_attn_gain, group_rank * shard_rows, shard_rows, 0
    )
    feedforward_gain_grad = lax.dynamic_slice_in_dim(
        sum_mlp_gain, group_rank * shard_rows, shard_rows, 0
    )
    return (
        layer_out,
        tokens_grad,
        attention_gain_grad,
        attn_grads[:, :proj_width],
        sum_head_gain,
        attn_grads[:, proj_width:],
        feedforward_gain_grad,
        mlp_grads[:, :ff_width],
        mlp_grads[:, ff_width : 2 * ff_width],
        mlp_grads[:, 2 * ff_width :],
    )


def solution(mesh):
    in_specs = (
        P(("rep", "seq", "ctx"), None),
        P(("rep", "seq", "ctx"), None),
        P(("rep", "seq")),
        P(("rep", "seq")),
        P(("seq", "ctx")),
        P(("seq", "ctx"), None),
        P(),
        P(("seq", "ctx"), None),
        P(("seq", "ctx")),
        P(("seq", "ctx"), None),
        P(("seq", "ctx"), None),
        P(("seq", "ctx"), None),
    )
    out_specs = (
        P(("rep", "seq", "ctx"), None),
        P(("rep", "seq", "ctx"), None),
        P(("seq", "ctx")),
        P(("seq", "ctx"), None),
        P(),
        P(("seq", "ctx"), None),
        P(("seq", "ctx")),
        P(("seq", "ctx"), None),
        P(("seq", "ctx"), None),
        P(("seq", "ctx"), None),
    )
    return jax.shard_map(
        per_device, mesh=mesh, in_specs=in_specs, out_specs=out_specs, check_vma=False
    )
```

profile of v0, /device:TPU:0, one launch (start us, length us, event | category | flops | bytes accessed | tf_op | source)
XLA Modules:
  0.0 4382.5 jit_solution(18146430784652032975)
XLA Ops:
  8.0 22.4 all-gather
  30.7 462.0 %all-gather.10.cloned.1.call-done = bf16[2048,6144]{1,0:T(8,128)(2,1)} async-done(((bf16[256,6144]{1,0:T(8,128)(2,1)}), bf16[2048,6144]{1,0:T(8,128)(2,1)}) %all-gather.10.cloned.1.call-update) | async-done | bytes 25165840 | tf_op jit(solution)/shard_map/all_gather | solution.py:98
  492.8 11.7 fusion.46
  516.4 20.9 all-gather.1
  545.0 10.4 all-gather.12.cloned.1.call-done
  557.7 45.0 %all-gather.14.cloned.1.call-done = bf16[1024,1024]{0,1:T(8,128)(2,1)} async-done(((bf16[256,1024]{0,1:T(8,128)(2,1)}), bf16[1024,1024]{0,1:T(8,128)(2,1)}) %all-gather.14.cloned.1.call-update) | async-done | bytes 2097168 | tf_op jit(solution)/shard_map/all_gather | solution.py:134
  602.7 12.2 fusion.56
  615.0 8.1 fusion.3
  623.1 7.6 divide_convert_fusion
  630.7 3.2 fusion.27
  636.6 3.9 multiply_convert_fusion.6
  640.5 87.4 %all-gather.16.cloned.1.call-done = bf16[2048,2048]{1,0:T(8,128)(2,1)} async-done(((bf16[256,2048]{1,0:T(8,128)(2,1)}), bf16[2048,2048]{1,0:T(8,128)(2,1)}) %all-gather.16.cloned.1.call-update) | async-done | bytes 8388624 | tf_op jit(solution)/shard_map/all_gather | solution.py:166
  727.9 6.2 multiply_reduce_fusion.3
  734.4 473.5 %all-gather.18.cloned.1.call-done = bf16[2048,6144]{1,0:T(8,128)(2,1)} async-done(((bf16[256,6144]{1,0:T(8,128)(2,1)}), bf16[2048,6144]{1,0:T(8,128)(2,1)}) %all-gather.18.cloned.1.call-update) | async-done | bytes 25165840 | tf_op jit(solution)/shard_map/all_gather | solution.py:176
  1207.9 14.3 fusion.57
  1222.2 468.7 %all-gather.20.cloned.1.call-done = bf16[2048,6144]{1,0:T(8,128)(2,1)} async-done(((bf16[256,6144]{1,0:T(8,128)(2,1)}), bf16[2048,6144]{1,0:T(8,128)(2,1)}) %all-gather.20.cloned.1.call-update) | async-done | bytes 25165840 | tf_op jit(solution)/shard_map/all_gather | solution.py:177
  1690.9 14.3 fusion.58
  1705.3 468.9 %all-gather.22.cloned.1.call-done = bf16[2048,6144]{1,0:T(8,128)(2,1)} async-done(((bf16[256,6144]{1,0:T(8,128)(2,1)}), bf16[2048,6144]{1,0:T(8,128)(2,1)}) %all-gather.22.cloned.1.call-update) | async-done | bytes 25165840 | tf_op jit(solution)/shard_map/all_gather | solution.py:196
  2174.1 19.1 multiply_convert_fusion
  2193.2 13.5 fusion.59
  2206.7 15.2 multiply_reduce_fusion
  2224.4 8.6 multiply_convert_fusion.3
  2234.1 14.6 fusion
  2251.1 10.1 fusion.2
  2261.3 7.7 fusion.5
  2270.3 7.5 bitcast_convert_fusion
  2277.8 4.1 copy.117
  2282.0 4.7 convolution_multiply_fusion
  2298.6 4.8 fusion.22
  2303.4 5.7 convolution_convert_fusion.4
  2309.1 5.0 reduce-scatter.5.cloned.1.call-done
  2325.4 34.5 reduce-scatter.7.cloned.1.call-done
  2359.9 12.6 convolution_convert_fusion.3
  2372.5 22.9 pad_maximum_fusion.1
  2396.6 13.9 convolution_convert_fusion.1
  2410.5 14.0 convolution_convert_fusion.2
  2424.5 14.2 convolution_convert_fusion
  2438.7 50.8 %pad_maximum_fusion = bf16[2048,18432]{1,0:T(8,128)(2,1)} fusion(bf16[2048,6144]{1,0:T(8,128)(2,1)} %convolution_convert_fusion, bf16[2048,6144]{1,0:T(8,128)(2,1)} %convolution_convert_fusion.1, bf16[2048,6144]{1,0:T(8,128)(2,1)} %convolution_convert_fusion.2), kind=kLoop, calls=%fused_computation | loop fusion | flops 226492416 | bytes 150994944 | tf_op jit(solution)/shard_map/concatenate | solution.py:223
  2489.5 448.2 %reduce-scatter.9.cloned.1.call-done = bf16[256,8192]{1,0:T(8,128)(2,1)} async-done(((bf16[2048,8192]{1,0:T(8,128)(2,1)}), bf16[256,8192]{1,0:T(8,128)(2,1)}) %reduce-scatter.9.cloned.1.call-update) | async-done | bytes 4194320 | tf_op jit(solution)/shard_map/reduce_scatter | solution.py:318
  2937.7 1180.7 %reduce-scatter.11.cloned.1.call-done = bf16[256,18432]{1,0:T(8,128)(2,1)} async-done(((bf16[2048,18432]{1,0:T(8,128)(2,1)}), bf16[256,18432]{1,0:T(8,128)(2,1)}) %reduce-scatter.11.cloned.1.call-update) | async-done | bytes 9437200 | tf_op jit(solution)/shard_map/reduce_scatter | solution.py:222
  4120.0 15.0 fusion.10
  4135.1 14.9 fusion.17
  4150.0 40.8 all-reduce
  4192.0 3.2 fusion.16
  4195.1 164.5 %all-reduce.4.cloned.1.call-done = (bf16[256,8192]{1,0:T(8,128)(2,1)}, bf16[256,18432]{1,0:T(8,128)(2,1)}) async-done(((bf16[256,8192]{1,0:T(8,128)(2,1)}, bf16[256,18432]{1,0:T(8,128)(2,1)}), (bf16[256,8192]{1,0:T(8,128)(2,1)}, bf16[256,18432]{1,0:T(8,128)(2,1)})) %all-reduce.4.cloned.1.call-update) | async-done | bytes 13631504 | tf_op jit(solution)/shard_map/psum | solution.py:67
  4359.7 5.9 slice.91
  4365.6 2.8 slice.92
  4368.4 6.9 fusion.53
  (213 shorter events, 59.9 us)
Async XLA Ops:
  7.2 23.2 copy-start.16
  7.2 485.6 %all-gather.10.cloned.1.call-start = ((), (), s32[]{:S(2)}) async-start(), calls=%async_computation.4 | async-start | bytes 28311552 | tf_op jit(solution)/shard_map/all_gather | solution.py:98
  7.9 547.5 %all-gather.12.cloned.1.call-start = ((), (), s32[]{:S(2)}) async-start(), calls=%async_computation.5 | async-start | bytes 2621440 | tf_op jit(solution)/shard_map/all_gather | solution.py:135
  30.4 474.1 %copy-start.36 = (f32[8,1,256]{2,1,0:T(1,128)}, f32[8,1,256]{2,1,0:T(1,128)S(1)}, u32[]{:S(2)}) copy-start(f32[8,1,256]{2,1,0:T(1,128)S(1)} %convert_element_type.136) | copy-start | bytes 24580
  30.7 473.8 %copy-start.38 = (f32[256]{0:T(256)}, f32[256]{0:T(256)S(1)}, u32[]{:S(2)}) copy-start(f32[256]{0:T(256)S(1)} %add_rsqrt_fusion.3) | copy-start | bytes 3076
  492.8 15.4 copy-start.55
  508.1 94.6 %all-gather.14.cloned.1.call-start = ((), (), s32[]{:S(2)}) async-start(), calls=%async_computation.6 | async-start | bytes 2621440 | tf_op jit(solution)/shard_map/all_gather | solution.py:134
  508.2 32.9 copy-start.49
  508.8 33.9 copy-start.27
  508.8 33.9 copy-start.29
  513.8 214.1 %all-gather.16.cloned.1.call-start = ((), (), s32[]{:S(2)}) async-start(), calls=%async_computation.7 | async-start | bytes 9437184 | tf_op jit(solution)/shard_map/all_gather | solution.py:166
  514.4 693.5 %all-gather.18.cloned.1.call-start = ((), (), s32[]{:S(2)}) async-start(), calls=%async_computation.8 | async-start | bytes 28311552 | tf_op jit(solution)/shard_map/all_gather | solution.py:176
  515.0 22.3 copy-start.52
  515.0 22.4 copy-start.53
  515.0 1175.9 %all-gather.20.cloned.1.call-start = ((), (), s32[]{:S(2)}) async-start(), calls=%async_computation.9 | async-start | bytes 28311552 | tf_op jit(solution)/shard_map/all_gather | solution.py:177
  515.6 1658.5 %all-gather.22.cloned.1.call-start = ((), (), s32[]{:S(2)}) async-start(), calls=%async_computation.10 | async-start | bytes 28311552 | tf_op jit(solution)/shard_map/all_gather | solution.py:196
  516.3 1797.7 %reduce-scatter.5.cloned.1.call-start = ((), (), s32[]{:S(2)}) async-start(), calls=%async_computation.11 | async-start | bytes 2621440 | tf_op jit(solution)/shard_map/reduce_scatter | solution.py:274
  543.7 59.0 %copy-start.14 = (bf16[256,16,64]{2,0,1:T(8,128)(2,1)}, bf16[256,16,64]{2,0,1:T(8,128)(2,1)S(1)}, u32[]{:S(2)}) copy-start(bf16[256,16,64]{2,0,1:T(8,128)(2,1)S(1)} %copy.80) | copy-start | bytes 1572868
  557.7 73.0 %copy-start.7 = (bf16[128,8,8,128]{3,2,1,0:T(8,128)(2,1)}, bf16[128,8,8,128]{3,2,1,0:T(8,128)(2,1)S(1)}, u32[]{:S(2)}) copy-start(bf16[128,8,8,128]{3,2,1,0:T(8,128)(2,1)S(1)} %copy.123) | copy-start | bytes 6291460
  615.0 8.1 copy-start.40
  636.6 91.3 %copy-start.17 = (bf16[256,2048]{1,0:T(8,128)(2,1)S(1)}, bf16[256,2048]{1,0:T(8,128)(2,1)}, u32[]{:S(2)}) copy-start(bf16[256,2048]{1,0:T(8,128)(2,1)} %param.12) | copy-start | bytes 3145732
  734.1 1487.8 %copy-start.19 = (f32[256,2048]{1,0:T(8,128)}, f32[256,2048]{1,0:T(8,128)S(1)}, u32[]{:S(2)}) copy-start(f32[256,2048]{1,0:T(8,128)S(1)} %get-tuple-element.54) | copy-start | bytes 6291460
  734.4 956.6 %copy-start.11 = (bf16[256,2048]{1,0:T(8,128)(2,1)}, bf16[256,2048]{1,0:T(8,128)(2,1)S(1)}, u32[]{:S(2)}) copy-start(bf16[256,2048]{1,0:T(8,128)(2,1)S(1)} %multiply_convert_fusion.5) | copy-start | bytes 3145732
  2206.7 15.2 copy-start.23
  2224.3 8.6 copy-start.4
  2224.3 9.1 copy-start.41
  2224.3 9.1 copy-start.43
  2234.1 14.7 slice-start
  2234.1 14.7 slice-start.1
  2234.1 15.9 slice-start.2
  2234.1 17.1 slice-start.3
  2251.1 10.1 copy-start.15
  2261.3 7.8 copy-start.48
  2261.3 8.4 copy-start.50
  2269.0 90.8 %reduce-scatter.7.cloned.1.call-start = ((), (), s32[]{:S(2)}) async-start(), calls=%async_computation.12 | async-start | bytes 2621440 | tf_op jit(solution)/shard_map/reduce_scatter | solution.py:280
  2281.9 655.8 %reduce-scatter.9.cloned.1.call-start = ((), (), s32[]{:S(2)}) async-start(), calls=%async_computation.13 | async-start | bytes 37748736 | tf_op jit(solution)/shard_map/reduce_scatter | solution.py:318
  2303.4 56.5 %copy-start.25 = (bf16[256,2048]{1,0:T(8,128)(2,1)}, bf16[256,2048]{1,0:T(8,128)(2,1)S(1)}, u32[]{:S(2)}) copy-start(bf16[256,2048]{1,0:T(8,128)(2,1)S(1)} %get-tuple-element.27) | copy-start | bytes 3145732
  2322.3 37.6 copy-start.18
  2322.3 37.6 copy-start.37
  2322.3 37.6 copy-start.39
  2325.3 47.1 %copy-start.31 = (bf16[256,1024]{1,0:T(8,128)(2,1)}, bf16[256,1024]{1,0:T(8,128)(2,1)S(1)}, u32[]{:S(2)}) copy-start(bf16[256,1024]{1,0:T(8,128)(2,1)S(1)} %get-tuple-element.32) | copy-start | bytes 1572868
  2395.4 1723.1 %reduce-scatter.11.cloned.1.call-start = ((), (), s32[]{:S(2)}) async-start(), calls=%async_computation.14 | async-start | bytes 84934656 | tf_op jit(solution)/shard_map/reduce_scatter | solution.py:222
  2410.5 14.0 copy-start.24
  2489.5 1870.2 %all-reduce.4.cloned.1.call-start = ((), (), s32[]{:S(2)}) async-start(), calls=%async_computation.15 | async-start | bytes 27262976 | tf_op jit(solution)/shard_map/psum | solution.py:67
  4120.0 15.0 copy-start.45
  4135.1 14.9 copy-start.51
  4135.1 56.9 %copy-start.6 = (f32[256,2048]{1,0:T(8,128)S(1)}, f32[256,2048]{1,0:T(8,128)}, u32[]{:S(2)}) copy-start(f32[256,2048]{1,0:T(8,128)} %copy-done.4) | copy-start | bytes 6291460
  4359.7 8.7 copy-start.1
  (25 other events, 75.0 us)
Sparse Core Ops, SparseCore 0:
  9.6 483.1 all-gather.9
  508.2 47.1 all-gather.11
  557.6 45.0 all-gather.13
  604.7 123.1 all-gather.15
  729.3 478.5 all-gather.17
  1209.3 481.6 all-gather.19
  1692.5 481.6 all-gather.21
  2269.1 44.8 reduce-scatter.4
  2316.5 43.3 reduce-scatter.6
  2395.5 542.1 reduce-scatter.8
  2941.6 1176.8 reduce-scatter.10
  4121.1 238.5 all-reduce.3
where the time goes:
time: 4390 us; the launch traced here: 4380 us
  waiting for transfers between devices  3850 us (88%)
  matrix products  243 us (6%)
  other arithmetic  130 us (3%)
  blocking collectives  84 us (2%)
  local copies, waits for them, and re-layouts  57.2 us (1%)
    reduce_scatter x1, waiting for transfers between devices, per_device(): lax.psum_scatter(jnp.concatenate([lax.dot_general(normed_rows, d_gate_low...  1180 us
    all_gather x1, waiting for transfers between devices, per_device(): gate_piece = lax.all_gather(gate_weight, ('seq', 'ctx'), axis=0, tiled=True)  474 us
    all_gather x1, waiting for transfers between devices, per_device(): lax.all_gather(down_weight, ('seq', 'ctx'), axis=0, tiled=True)  469 us
    all_gather x1, waiting for transfers between devices, per_device(): up_piece = lax.all_gather(up_weight, ('seq', 'ctx'), axis=0, tiled=True)  469 us
    all_gather x1, waiting for transfers between devices, per_device(): lax.all_gather(projection_weight, ('seq', 'ctx'), axis=0, tiled=True)  462 us
    reduce_scatter x1, waiting for transfers between devices, per_device(): lax.psum_scatter(jnp.concatenate([lax.dot_general(normed_rows, d_proj_low...  448 us
    psum x1, waiting for transfers between devices, over_replicas(): lax.psum(grad_parts[1].astype(jnp.bfloat16), 'rep').astype(jnp.float32)  165 us
  transfers between devices with their start and end apart: 12, of which 12 were waited for; matrix products, arithmetic and copies ran while one was open for 6% of the time, Pallas kernels for 0%

commit v1 on v0

--- a/solution.py
+++ b/solution.py
@@ -11,6 +11,19 @@
 masked_value = -1e30
 contract_rows = (((0,), (0,)), ((), ()))
 contract_cols = (((1,), (1,)), ((), ()))
+
+
+def ring_gather(value, axis, dim):
+    ways = lax.axis_size(axis)
+    up = [(d, (d + 1) % ways) for d in range(ways)]
+    down = [(d, (d - 1) % ways) for d in range(ways)]
+    earlier, later = ([value], [value])
+    for _ in range(ways // 2):
+        earlier.append(lax.ppermute(earlier[-1], axis, up))
+    for _ in range((ways - 1) // 2):
+        later.append(lax.ppermute(later[-1], axis, down))
+    line = jnp.concatenate([*earlier[::-1], *later[1:]], axis=dim)
+    return jnp.roll(line, (lax.axis_index(axis) - ways // 2) * value.shape[dim], axis=dim)
 
 
 def rope_tables(positions):
@@ -173,7 +186,7 @@
     root_mlp = lax.rsqrt(jnp.mean(resid_mid * resid_mid, axis=1, keepdims=True) + norm_epsilon)
     unit_mlp = resid_mid * root_mlp
     gain_piece = lax.all_gather(feedforward_gain, ("seq", "ctx"), axis=0, tiled=True)
-    gate_piece = lax.all_gather(gate_weight, ("seq", "ctx"), axis=0, tiled=True)
+    gate_piece = ring_gather(gate_weight, ("seq", "ctx"), 0)
     up_piece = lax.all_gather(up_weight, ("seq", "ctx"), axis=0, tiled=True)
     columns = unit_mlp
     normed = (columns * gain_piece.astype(jnp.float32)).astype(jnp.bfloat16)

time: 4390 us -> 4820 us (1.098)
  starting transfers between devices: 0.48 us -> 318 us
  blocking collectives: 84 us -> 200 us
  waiting for transfers between devices: 3850 us -> 3800 us
  local copies, waits for them, and re-layouts: 57.2 us -> 106 us
    ppermute x0 -> x7, waiting for transfers between devices: none -> 489 us  [the longest x4 412 us: ring_gather(): earlier.append(lax.ppermute(earlier[-1], axis, up))]
    all_gather x1, waiting for transfers between devices: 469 us -> 0.01 us  [per_device(): lax.all_gather(down_weight, ('seq', 'ctx'), axis=0, tiled=True)]
    ppermute x0 -> x7, starting transfers between devices: none -> 317 us  [the longest x4 311 us: ring_gather(): earlier.append(lax.ppermute(earlier[-1], axis, up))]
    all_gather x1, blocking collectives: 20.9 us -> 136 us  [per_device(): lax.all_gather(feedforward_gain, ('seq', 'ctx'), axis=0, tiled=True)]
  transfers between devices with their start and end apart: 12 -> 19, of which waited for: 12 -> 14; matrix products, arithmetic and copies ran while one was open for 6% -> 7% of each run, Pallas kernels for 0% -> 0%
where the time goes in v1:
time: 4820 us; the launch traced here: 4810 us
  waiting for transfers between devices  3800 us (79%)
  starting transfers between devices  318 us (7%)
  matrix products  243 us (5%)
  blocking collectives  200 us (4%)
  other arithmetic  131 us (3%)
  local copies, waits for them, and re-layouts  106 us (2%)
    reduce_scatter x1, waiting for transfers between devices, per_device(): lax.psum_scatter(jnp.concatenate([lax.dot_general(normed_rows, d_gate_low...  1180 us
    all_gather x1, waiting for transfers between devices, per_device(): up_piece = lax.all_gather(up_weight, ('seq', 'ctx'), axis=0, tiled=True)  474 us
    all_gather x1, waiting for transfers between devices, per_device(): lax.all_gather(projection_weight, ('seq', 'ctx'), axis=0, tiled=True)  461 us
    all_gather x1, waiting for transfers between devices, per_device(): gate_piece = lax.all_gather(gate_weight, ('seq', 'ctx'), axis=0, tiled=True)  450 us
    reduce_scatter x1, waiting for transfers between devices, per_device(): lax.psum_scatter(jnp.concatenate([lax.dot_general(normed_rows, d_proj_low...  449 us
    ppermute x4, waiting for transfers between devices, ring_gather(): earlier.append(lax.ppermute(earlier[-1], axis, up))  412 us
    ppermute x4, starting transfers between devices, ring_gather(): earlier.append(lax.ppermute(earlier[-1], axis, up))  311 us
    psum x1, waiting for transfers between devices, over_replicas(): lax.psum(grad_parts[1].astype(jnp.bfloat16), 'rep').astype(jnp.float32)  165 us
  transfers between devices with their start and end apart: 19, of which 14 were waited for; matrix products, arithmetic and copies ran while one was open for 7% of the time, Pallas kernels for 0%

profile of v1, /device:TPU:0, one launch (start us, length us, event | category | flops | bytes accessed | tf_op | source)
XLA Modules:
  0.0 4809.9 jit_solution(17004080988189481351)
XLA Ops:
  8.8 22.5 all-gather
  31.6 461.2 %all-gather.10.cloned.1.call-done = bf16[2048,6144]{1,0:T(8,128)(2,1)} async-done(((bf16[256,6144]{1,0:T(8,128)(2,1)}), bf16[2048,6144]{1,0:T(8,128)(2,1)}) %all-gather.10.cloned.1.call-update) | async-done | bytes 25165840 | tf_op jit(solution)/shard_map/all_gather | solution.py:111
  492.8 11.7 fusion.48
  517.8 139.2 %collective-permute-done = bf16[256,6144]{1,0:T(8,128)(2,1)S(1)} collective-permute-done((bf16[256,6144]{1,0:T(8,128)(2,1)S(1)}, bf16[256,6144]{1,0:T(8,128)(2,1)S(1)}, u32[]{:S(2)}, u32[]{:S(2)}) %collective-permute-start) | collective-permute-done | bytes 3145760 | tf_op jit(solution)/shard_map/ppermute | solution.py:22
  657.0 61.0 %collective-permute-start.1 = (bf16[256,6144]{1,0:T(8,128)(2,1)S(1)}, bf16[256,6144]{1,0:T(8,128)(2,1)S(1)}, u32[]{:S(2)}, u32[]{:S(2)}) collective-permute-start(bf16[256,6144]{1,0:T(8,128)(2,1)S(1)} %collective-permute-done), channel_id=1, source_target_pairs={{0,1},{1,2},{2,3},{3,4},{4,5},{5,6},{6,7},{7,0},{8,9},{9,10},{10,1... | collective-permute-start | bytes 9437192 | tf_op jit(solution)/shard_map/ppermute | solution.py:22
  719.8 136.3 %collective-permute-done.1 = bf16[256,6144]{1,0:T(8,128)(2,1)S(1)} collective-permute-done((bf16[256,6144]{1,0:T(8,128)(2,1)S(1)}, bf16[256,6144]{1,0:T(8,128)(2,1)S(1)}, u32[]{:S(2)}, u32[]{:S(2)}) %collective-permute-start.1) | collective-permute-done | bytes 3145760 | tf_op jit(solution)/shard_map/ppermute | solution.py:22
  856.1 123.3 %collective-permute-start.2 = (bf16[256,6144]{1,0:T(8,128)(2,1)S(1)}, bf16[256,6144]{1,0:T(8,128)(2,1)}, u32[]{:S(2)}, u32[]{:S(2)}) collective-permute-start(bf16[256,6144]{1,0:T(8,128)(2,1)S(1)} %collective-permute-done.1), channel_id=1, source_target_pairs={{0,1},{1,2},{2,3},{3,4},{4,5},{5,6},{6,7},{7,0},{8,9},{9,10},{10,1... | collective-permute-start | bytes 9437192 | tf_op jit(solution)/shard_map/ppermute | solution.py:22
  979.3 13.0 collective-permute-done.4
  994.6 136.4 %collective-permute-done.2 = bf16[256,6144]{1,0:T(8,128)(2,1)} collective-permute-done((bf16[256,6144]{1,0:T(8,128)(2,1)S(1)}, bf16[256,6144]{1,0:T(8,128)(2,1)}, u32[]{:S(2)}, u32[]{:S(2)}) %collective-permute-start.2) | collective-permute-done | bytes 3145760 | tf_op jit(solution)/shard_map/ppermute | solution.py:22
  1130.9 125.6 %collective-permute-start.3 = (bf16[256,6144]{1,0:T(8,128)(2,1)}, bf16[256,6144]{1,0:T(8,128)(2,1)}, u32[]{:S(2)}, u32[]{:S(2)}) collective-permute-start(bf16[256,6144]{1,0:T(8,128)(2,1)} %collective-permute-done.2), channel_id=1, source_target_pairs={{0,1},{1,2},{2,3},{3,4},{4,5},{5,6},{6,7},{7,0},{8,9},{9,10},{10,1... | collective-permute-start | bytes 9437192 | tf_op jit(solution)/shard_map/ppermute | solution.py:22
  1256.5 136.3 %all-gather.1 = bf16[8,1,256]{2,1,0:T(2,128)(2,1)S(1)} all-gather(bf16[1,1,256]{2,1,0:T(2,128)(2,1)S(1)} %reshape.310), channel_id=1, replica_groups=mesh['rep'=4,'seq'=2,'ctx'=4] {'seq','ctx'}, dimensions={0}, use_global_device_ids=true | all-gather | bytes 4608 | tf_op jit(solution)/shard_map/all_gather | solution.py:188
  1418.9 64.2 %collective-permute-done.6 = bf16[256,6144]{1,0:T(8,128)(2,1)S(1)} collective-permute-done((bf16[256,6144]{1,0:T(8,128)(2,1)}, bf16[256,6144]{1,0:T(8,128)(2,1)S(1)}, u32[]{:S(2)}, u32[]{:S(2)}) %collective-permute-start.6) | collective-permute-done | bytes 3145760 | tf_op jit(solution)/shard_map/ppermute | solution.py:24
  1515.3 14.5 fusion.45
  1532.1 12.8 fusion.59
  1544.9 8.1 fusion.5
  1553.1 7.6 divide_convert_fusion
  1570.5 86.3 %all-gather.16.cloned.1.call-done = bf16[2048,2048]{1,0:T(8,128)(2,1)} async-done(((bf16[256,2048]{1,0:T(8,128)(2,1)}), bf16[2048,2048]{1,0:T(8,128)(2,1)}) %all-gather.16.cloned.1.call-update) | async-done | bytes 8388624 | tf_op jit(solution)/shard_map/all_gather | solution.py:179
  1656.8 6.2 multiply_reduce_fusion.3
  1663.3 473.5 %all-gather.18.cloned.1.call-done = bf16[2048,6144]{1,0:T(8,128)(2,1)} async-done(((bf16[256,6144]{1,0:T(8,128)(2,1)}), bf16[2048,6144]{1,0:T(8,128)(2,1)}) %all-gather.18.cloned.1.call-update) | async-done | bytes 25165840 | tf_op jit(solution)/shard_map/all_gather | solution.py:190
  2136.8 11.6 fusion.60
  2148.5 21.2 multiply_convert_fusion
  2169.7 450.3 %all-gather.22.cloned.1.call-done = bf16[2048,6144]{1,0:T(8,128)(2,1)} async-done(((bf16[256,6144]{1,0:T(8,128)(2,1)}), bf16[2048,6144]{1,0:T(8,128)(2,1)}) %all-gather.22.cloned.1.call-update) | async-done | bytes 25165840 | tf_op jit(solution)/shard_map/all_gather | solution.py:227
  2620.0 13.6 fusion.61
  2633.7 14.9 multiply_reduce_fusion
  2651.0 8.5 multiply_convert_fusion.3
  2660.7 14.6 fusion.2
  2677.7 10.3 fusion.4
  2688.0 7.7 fusion.7
  2697.0 7.5 bitcast_convert_fusion
  2708.7 4.7 convolution_multiply_fusion
  2725.5 4.8 fusion.24
  2730.3 5.6 convolution_convert_fusion.4
  2736.0 5.0 reduce-scatter.5.cloned.1.call-done
  2752.2 34.3 reduce-scatter.7.cloned.1.call-done
  2786.5 12.6 convolution_convert_fusion.3
  2799.1 22.8 pad_maximum_fusion.1
  2823.2 13.9 convolution_convert_fusion.1
  2837.1 14.0 convolution_convert_fusion.2
  2851.1 14.2 convolution_convert_fusion
  2865.2 50.8 %pad_maximum_fusion = bf16[2048,18432]{1,0:T(8,128)(2,1)} fusion(bf16[2048,6144]{1,0:T(8,128)(2,1)} %convolution_convert_fusion, bf16[2048,6144]{1,0:T(8,128)(2,1)} %convolution_convert_fusion.1, bf16[2048,6144]{1,0:T(8,128)(2,1)} %convolution_convert_fusion.2), kind=kLoop, calls=%fused_computation | loop fusion | flops 226492416 | bytes 150994944 | tf_op jit(solution)/shard_map/concatenate | solution.py:236
  2916.1 448.7 %reduce-scatter.9.cloned.1.call-done = bf16[256,8192]{1,0:T(8,128)(2,1)} async-done(((bf16[2048,8192]{1,0:T(8,128)(2,1)}), bf16[256,8192]{1,0:T(8,128)(2,1)}) %reduce-scatter.9.cloned.1.call-update) | async-done | bytes 4194320 | tf_op jit(solution)/shard_map/reduce_scatter | solution.py:331
  3364.8 1181.3 %reduce-scatter.11.cloned.1.call-done = bf16[256,18432]{1,0:T(8,128)(2,1)} async-done(((bf16[2048,18432]{1,0:T(8,128)(2,1)}), bf16[256,18432]{1,0:T(8,128)(2,1)}) %reduce-scatter.11.cloned.1.call-update) | async-done | bytes 9437200 | tf_op jit(solution)/shard_map/reduce_scatter | solution.py:235
  4547.6 14.9 fusion.12
  4562.6 14.9 fusion.19
  4577.5 40.7 all-reduce
  4622.7 164.6 %all-reduce.4.cloned.1.call-done = (bf16[256,8192]{1,0:T(8,128)(2,1)}, bf16[256,18432]{1,0:T(8,128)(2,1)}) async-done(((bf16[256,8192]{1,0:T(8,128)(2,1)}, bf16[256,18432]{1,0:T(8,128)(2,1)}), (bf16[256,8192]{1,0:T(8,128)(2,1)}, bf16[256,18432]{1,0:T(8,128)(2,1)})) %all-reduce.4.cloned.1.call-update) | async-done | bytes 13631504 | tf_op jit(solution)/shard_map/psum | solution.py:80
  4787.3 5.9 slice.91
  4796.0 6.9 fusion.56
  (257 shorter events, 134.1 us)
Async XLA Ops:
  7.2 24.1 copy-start.21
  7.2 485.6 %all-gather.10.cloned.1.call-start = ((), (), s32[]{:S(2)}) async-start(), calls=%async_computation.4 | async-start | bytes 28311552 | tf_op jit(solution)/shard_map/all_gather | solution.py:111
  7.9 1507.4 %all-gather.20.cloned.1.call-start = ((), (), s32[]{:S(2)}) async-start(), calls=%async_computation.9 | async-start | bytes 28311552 | tf_op jit(solution)/shard_map/all_gather | solution.py:209
  8.7 1521.1 %all-gather.12.cloned.1.call-start = ((), (), s32[]{:S(2)}) async-start(), calls=%async_computation.5 | async-start | bytes 2621440 | tf_op jit(solution)/shard_map/all_gather | solution.py:148
  31.3 473.2 %copy-start.43 = (f32[8,1,256]{2,1,0:T(1,128)}, f32[8,1,256]{2,1,0:T(1,128)S(1)}, u32[]{:S(2)}) copy-start(f32[8,1,256]{2,1,0:T(1,128)S(1)} %convert_element_type.136) | copy-start | bytes 24580
  31.6 472.9 %copy-start.45 = (f32[256]{0:T(256)}, f32[256]{0:T(256)S(1)}, u32[]{:S(2)}) copy-start(f32[256]{0:T(256)S(1)} %add_rsqrt_fusion.3) | copy-start | bytes 3076
  492.8 15.4 copy-start.62
  508.1 1024.0 %all-gather.14.cloned.1.call-start = ((), (), s32[]{:S(2)}) async-start(), calls=%async_computation.6 | async-start | bytes 2621440 | tf_op jit(solution)/shard_map/all_gather | solution.py:147
  508.3 1003.1 %copy-start.56 = (f32[128]{0:T(128)}, f32[128]{0:T(128)S(1)}, u32[]{:S(2)}) copy-start(f32[128]{0:T(128)S(1)} %get-tuple-element.49) | copy-start | bytes 1540
  508.8 1004.1 %copy-start.33 = (f32[256,64]{1,0:T(8,128)}, f32[256,64]{1,0:T(8,128)S(1)}, u32[]{:S(2)}) copy-start(f32[256,64]{1,0:T(8,128)S(1)} %get-tuple-element.47) | copy-start | bytes 196612
  508.8 1004.1 %copy-start.35 = (f32[256,64]{1,0:T(8,128)}, f32[256,64]{1,0:T(8,128)S(1)}, u32[]{:S(2)}) copy-start(f32[256,64]{1,0:T(8,128)S(1)} %get-tuple-element.48) | copy-start | bytes 196612
  513.8 1143.0 %all-gather.16.cloned.1.call-start = ((), (), s32[]{:S(2)}) async-start(), calls=%async_computation.7 | async-start | bytes 9437184 | tf_op jit(solution)/shard_map/all_gather | solution.py:179
  514.4 742.1 %copy-start.63 = (bf16[256]{0:T(256)(128)(2,1)S(1)}, bf16[256]{0:T(256)(128)(2,1)}, u32[]{:S(2)}) copy-start(bf16[256]{0:T(256)(128)(2,1)} %param.20) | copy-start | bytes 1540
  514.4 878.5 %copy-start.59 = (s32[1024]{0:T(1024)S(1)}, s32[1024]{0:T(1024)}, u32[]{:S(2)}) copy-start(s32[1024]{0:T(1024)} %param.14) | copy-start | bytes 12292
  514.4 878.5 %copy-start.60 = (s32[1024]{0:T(1024)S(1)}, s32[1024]{0:T(1024)}, u32[]{:S(2)}) copy-start(s32[1024]{0:T(1024)} %param.15) | copy-start | bytes 12292
  514.4 1622.4 %all-gather.18.cloned.1.call-start = ((), (), s32[]{:S(2)}) async-start(), calls=%async_computation.8 | async-start | bytes 28311552 | tf_op jit(solution)/shard_map/all_gather | solution.py:190
  515.0 2105.0 %all-gather.22.cloned.1.call-start = ((), (), s32[]{:S(2)}) async-start(), calls=%async_computation.10 | async-start | bytes 28311552 | tf_op jit(solution)/shard_map/all_gather | solution.py:227
  515.8 2225.2 %reduce-scatter.5.cloned.1.call-start = ((), (), s32[]{:S(2)}) async-start(), calls=%async_computation.11 | async-start | bytes 2621440 | tf_op jit(solution)/shard_map/reduce_scatter | solution.py:287
  516.3 140.7 %collective-permute-start = (bf16[256,6144]{1,0:T(8,128)(2,1)S(1)}, bf16[256,6144]{1,0:T(8,128)(2,1)S(1)}, u32[]{:S(2)}, u32[]{:S(2)}) collective-permute-start(bf16[256,6144]{1,0:T(8,128)(2,1)S(1)} %copy-done.4), channel_id=1, source_target_pairs={{0,1},{1,2},{2,3},{3,4},{4,5},{5,6},{6,7},{7,0},{8,9},{9,10},{10,1... | collective-permute-start | bytes 9437192 | tf_op jit(solution)/shard_map/ppermute | solution.py:22
  657.0 335.3 %copy-start.15 = (bf16[256,6144]{1,0:T(8,128)(2,1)}, bf16[256,6144]{1,0:T(8,128)(2,1)S(1)}, u32[]{:S(2)}) copy-start(bf16[256,6144]{1,0:T(8,128)(2,1)S(1)} %collective-permute-done) | copy-start | bytes 9437188
  657.0 199.1 %collective-permute-start.1 = (bf16[256,6144]{1,0:T(8,128)(2,1)S(1)}, bf16[256,6144]{1,0:T(8,128)(2,1)S(1)}, u32[]{:S(2)}, u32[]{:S(2)}) collective-permute-start(bf16[256,6144]{1,0:T(8,128)(2,1)S(1)} %collective-permute-done), channel_id=1, source_target_pairs={{0,1},{1,2},{2,3},{3,4},{4,5},{5,6},{6,7},{7,0},{8,9},{9,10},{10,1... | collective-permute-start | bytes 9437192 | tf_op jit(solution)/shard_map/ppermute | solution.py:22
  717.9 274.4 %collective-permute-start.4 = (bf16[256,6144]{1,0:T(8,128)(2,1)S(1)}, bf16[256,6144]{1,0:T(8,128)(2,1)}, u32[]{:S(2)}, u32[]{:S(2)}) collective-permute-start(bf16[256,6144]{1,0:T(8,128)(2,1)S(1)} %copy-done.4), channel_id=1, source_target_pairs={{0,7},{1,0},{2,1},{3,2},{4,3},{5,4},{6,5},{7,6},{8,15},{9,8},{10,9... | collective-permute-start | bytes 9437192 | tf_op jit(solution)/shard_map/ppermute | solution.py:24
  856.1 138.5 %copy-start.17 = (bf16[256,6144]{1,0:T(8,128)(2,1)}, bf16[256,6144]{1,0:T(8,128)(2,1)S(1)}, u32[]{:S(2)}) copy-start(bf16[256,6144]{1,0:T(8,128)(2,1)S(1)} %collective-permute-done.1) | copy-start | bytes 9437188
  856.1 274.9 %collective-permute-start.2 = (bf16[256,6144]{1,0:T(8,128)(2,1)S(1)}, bf16[256,6144]{1,0:T(8,128)(2,1)}, u32[]{:S(2)}, u32[]{:S(2)}) collective-permute-start(bf16[256,6144]{1,0:T(8,128)(2,1)S(1)} %collective-permute-done.1), channel_id=1, source_target_pairs={{0,1},{1,2},{2,3},{3,4},{4,5},{5,6},{6,7},{7,0},{8,9},{9,10},{10,1... | collective-permute-start | bytes 9437192 | tf_op jit(solution)/shard_map/ppermute | solution.py:22
  992.3 402.2 %collective-permute-start.5 = (bf16[256,6144]{1,0:T(8,128)(2,1)}, bf16[256,6144]{1,0:T(8,128)(2,1)}, u32[]{:S(2)}, u32[]{:S(2)}) collective-permute-start(bf16[256,6144]{1,0:T(8,128)(2,1)} %collective-permute-done.4), channel_id=1, source_target_pairs={{0,7},{1,0},{2,1},{3,2},{4,3},{5,4},{6,5},{7,6},{8,15},{9,8},{10,9... | collective-permute-start | bytes 9437192 | tf_op jit(solution)/shard_map/ppermute | solution.py:24
  1130.9 265.4 %collective-permute-start.3 = (bf16[256,6144]{1,0:T(8,128)(2,1)}, bf16[256,6144]{1,0:T(8,128)(2,1)}, u32[]{:S(2)}, u32[]{:S(2)}) collective-permute-start(bf16[256,6144]{1,0:T(8,128)(2,1)} %collective-permute-done.2), channel_id=1, source_target_pairs={{0,1},{1,2},{2,3},{3,4},{4,5},{5,6},{6,7},{7,0},{8,9},{9,10},{10,1... | collective-permute-start | bytes 9437192 | tf_op jit(solution)/shard_map/ppermute | solution.py:22
  1394.5 88.7 %collective-permute-start.6 = (bf16[256,6144]{1,0:T(8,128)(2,1)}, bf16[256,6144]{1,0:T(8,128)(2,1)S(1)}, u32[]{:S(2)}, u32[]{:S(2)}) collective-permute-start(bf16[256,6144]{1,0:T(8,128)(2,1)} %collective-permute-done.5), channel_id=1, source_target_pairs={{0,7},{1,0},{2,1},{3,2},{4,3},{5,4},{6,5},{7,6},{8,15},{9,8},{10,9... | collective-permute-start | bytes 9437192 | tf_op jit(solution)/shard_map/ppermute | solution.py:24
  1514.0 18.1 copy-start.19
  1532.1 28.7 copy-start.8
  1566.6 90.2 %copy-start.22 = (bf16[256,2048]{1,0:T(8,128)(2,1)S(1)}, bf16[256,2048]{1,0:T(8,128)(2,1)}, u32[]{:S(2)}) copy-start(bf16[256,2048]{1,0:T(8,128)(2,1)} %param.12) | copy-start | bytes 3145732
  1663.1 985.5 %copy-start.24 = (f32[256,2048]{1,0:T(8,128)}, f32[256,2048]{1,0:T(8,128)S(1)}, u32[]{:S(2)}) copy-start(f32[256,2048]{1,0:T(8,128)S(1)} %get-tuple-element.54) | copy-start | bytes 6291460
  1663.3 485.1 %copy-start.12 = (bf16[256,2048]{1,0:T(8,128)(2,1)}, bf16[256,2048]{1,0:T(8,128)(2,1)S(1)}, u32[]{:S(2)}) copy-start(bf16[256,2048]{1,0:T(8,128)(2,1)S(1)} %multiply_convert_fusion.5) | copy-start | bytes 3145732
  2633.7 14.9 copy-start.29
  2660.6 14.7 slice-start.1
  2660.6 15.9 slice-start.2
  2660.7 17.1 slice-start.3
  2695.8 90.8 %reduce-scatter.7.cloned.1.call-start = ((), (), s32[]{:S(2)}) async-start(), calls=%async_computation.12 | async-start | bytes 2621440 | tf_op jit(solution)/shard_map/reduce_scatter | solution.py:293
  2708.6 656.1 %reduce-scatter.9.cloned.1.call-start = ((), (), s32[]{:S(2)}) async-start(), calls=%async_computation.13 | async-start | bytes 37748736 | tf_op jit(solution)/shard_map/reduce_scatter | solution.py:331
  2730.3 56.2 %copy-start.31 = (bf16[256,2048]{1,0:T(8,128)(2,1)}, bf16[256,2048]{1,0:T(8,128)(2,1)S(1)}, u32[]{:S(2)}) copy-start(bf16[256,2048]{1,0:T(8,128)(2,1)S(1)} %get-tuple-element.27) | copy-start | bytes 3145732
  2749.1 37.4 copy-start.23
  2749.2 37.4 copy-start.44
  2749.2 37.4 copy-start.46
  2752.2 46.9 copy-start.38
  2822.0 1724.1 %reduce-scatter.11.cloned.1.call-start = ((), (), s32[]{:S(2)}) async-start(), calls=%async_computation.14 | async-start | bytes 84934656 | tf_op jit(solution)/shard_map/reduce_scatter | solution.py:235
  2916.0 1871.2 %all-reduce.4.cloned.1.call-start = ((), (), s32[]{:S(2)}) async-start(), calls=%async_computation.15 | async-start | bytes 27262976 | tf_op jit(solution)/shard_map/psum | solution.py:80
  4547.6 15.0 copy-start.53
  4562.6 14.9 copy-start.58
  4562.6 56.9 %copy-start.7 = (f32[256,2048]{1,0:T(8,128)S(1)}, f32[256,2048]{1,0:T(8,128)}, u32[]{:S(2)}) copy-start(f32[256,2048]{1,0:T(8,128)} %copy-done.5) | copy-start | bytes 6291460
  (39 other events, 184.0 us)
Sparse Core Ops, SparseCore 0:
  9.6 483.1 all-gather.9
  494.3 871.8 all-gather.19
  1368.4 65.2 all-gather.11
  1435.7 95.9 all-gather.13
  1533.6 123.1 all-gather.15
  1658.2 478.5 all-gather.17
  2138.4 481.6 all-gather.21
  2695.9 44.9 reduce-scatter.4
  2743.3 43.1 reduce-scatter.6
  2822.1 542.6 reduce-scatter.8
  3368.6 1177.3 reduce-scatter.10
  4548.7 238.5 all-reduce.3
